TPU v7x, 32 devices: a whole 2x2x4 slice. The times are simulated.
32 devices in a mesh: row: 4 (over z), col: 2 (over y), ex: 4 (over x, core).
Axes of the slice: x: 2, y: 2, z: 4, core: 2. Of those that a mesh axis runs over, the one named last changes fastest.
Arguments:
- train_in: bfloat16 [2048, 8192], P('ex', 'row'), may hold values from -6 to 6
- train_out: bfloat16 [2048, 8192], P('ex', 'col'), may hold values from -0.0047912598 to 0.0047912598
- query_in: bfloat16 [128, 8192], P('ex', 'row'), may hold values from -6 to 6
- query_out: bfloat16 [128, 8192], P('ex', 'col'), may hold values from -0.023925781 to 0.023925781
- query_ids: int32 [128], P('ex'), may hold values from 0 to 1
- in_basis: bfloat16 [8, 1024, 1024], P('row'), may hold values from -1 to 1, as said below
- out_basis: bfloat16 [8, 1024, 1024], P('col'), may hold values from -1 to 1, as said below
- level_table: float32 [64, 64], replicated, may hold values from 0.5 to 8
- in_level: int32 [8192], P('row'), may hold values from 0 to 63
- out_level: int32 [8192], P('col'), may hold values from 0 to 63
- lengths: int32 [4], replicated, may hold values from 1 to 1024, 2048 in all
Outputs:
- token_scores: float32 [2, 2048], P(None, 'ex')
- example_scores: float32 [2, 4], replicated
Inputs may be any that keep to these rules, and one draw needn't show every extreme that they name: `in_basis`: each block is an orthogonal matrix rounded to bfloat16. `out_basis`: each block is an orthogonal matrix rounded to bfloat16. `lengths`: the counts sum to 2048.
All inputs are finite; a program needn't handle non-finite values.
Results may differ from a plain program's by a relative error of at most 0.018.
Values may be sent and summed in bfloat16 or wider, within the bound.
A program may use at most 192 MiB of HBM per device.

v0:
```python
import jax
import jax.numpy as jnp
from jax import lax
from jax.sharding import PartitionSpec as P

QUERIES = 2


DAMPING = 0.1


def body(
    train_in,
    train_out,
    query_in,
    query_out,
    query_ids,
    in_basis,
    out_basis,
    level_table,
    in_level,
    out_level,
    lengths,
):
    highest = lax.Precision.HIGHEST
    ex_count = lax.axis_size("ex")
    ex_index = lax.axis_index("ex")
    in_sub = in_basis.shape[0]
    out_sub = out_basis.shape[0]
    width = in_basis.shape[1]
    per_query = in_sub * out_sub
    owned = QUERIES * per_query // ex_count
    block_ids = ex_index * owned + jnp.arange(owned, dtype=jnp.int32)
    query_of = block_ids % QUERIES
    pair_of = block_ids // QUERIES
    out_of = pair_of // in_sub
    in_of = pair_of % in_sub
    out_own = jnp.take(out_basis, out_of, axis=0)
    in_own = jnp.take(in_basis, in_of, axis=0)
    query_code = query_of.astype(jnp.float32)
    piece_in = lax.all_gather(query_in, "ex", axis=0, tiled=True)
    piece_out = lax.all_gather(query_out, "ex", axis=0, tiled=True)
    piece_ids = lax.all_gather(query_ids.astype(jnp.bfloat16), "ex", axis=0, tiled=True)
    count = piece_in.shape[0]
    chosen_in = jnp.take(piece_in.reshape(count, in_sub, width), in_of, axis=1)
    chosen_out = jnp.take(piece_out.reshape(count, out_sub, width), out_of, axis=1)
    weights = (piece_ids.astype(jnp.float32)[:, None] == query_code[None, :]).astype(jnp.bfloat16)
    chosen_out = chosen_out * weights[:, :, None]
    grad_own = jnp.einsum("mka,mkb->kab", chosen_out, chosen_in, preferred_element_type=jnp.float32)
    grad_own = grad_own.astype(jnp.bfloat16)
    half = jnp.einsum("kab,kac->kbc", out_own, grad_own, preferred_element_type=jnp.float32).astype(
        jnp.bfloat16
    )
    rotated = jnp.einsum("kbc,kcd->kbd", half, in_own, preferred_element_type=jnp.float32)
    levels = jnp.arange(level_table.shape[0], dtype=jnp.int32)
    out_levels = jnp.take(out_level.reshape(out_sub, width), out_of, axis=0)
    in_levels = jnp.take(in_level.reshape(in_sub, width), in_of, axis=0)
    out_onehot = (out_levels[:, :, None] == levels[None, None, :]).astype(jnp.float32)
    in_onehot = (in_levels[:, :, None] == levels[None, None, :]).astype(jnp.float32)
    partway = jnp.einsum("kbl,lm->kbm", out_onehot, level_table, precision=highest)
    eigen = jnp.einsum("kbm,kdm->kbd", partway, in_onehot, precision=highest)
    damped = (rotated / (eigen + DAMPING)).astype(jnp.bfloat16)
    back = jnp.einsum("kbd,kcd->kbc", damped, in_own, preferred_element_type=jnp.float32).astype(
        jnp.bfloat16
    )
    precond = jnp.einsum("kab,kbc->kac", out_own, back, preferred_element_type=jnp.float32).astype(
        jnp.bfloat16
    )
    tokens = train_in.shape[0]
    in_split = train_in.reshape(tokens, in_sub, width)
    out_split = train_out.reshape(tokens, out_sub, width)
    query_range = jnp.arange(QUERIES, dtype=jnp.int32)
    piece = lax.all_gather(precond, "ex", axis=0, tiled=True)

    def score_one(step, running):
        pair = step // QUERIES
        matrix = lax.dynamic_index_in_dim(piece, step, 0, keepdims=False)
        acts = lax.dynamic_index_in_dim(in_split, pair % in_sub, 1, keepdims=False)
        grads = lax.dynamic_index_in_dim(out_split, pair // in_sub, 1, keepdims=False)
        image = lax.dot_general(
            acts, matrix, (((1,), (1,)), ((), ())), preferred_element_type=jnp.float32
        )
        values = jnp.sum(image * grads.astype(jnp.float32), axis=1)
        selector = (query_range == step % QUERIES).astype(jnp.float32)
        return running + selector[:, None] * values[None, :]

    token_part = lax.fori_loop(
        0, piece.shape[0], score_one, jnp.zeros((QUERIES, tokens), jnp.float32)
    )
    token_scores = lax.psum(token_part, ("row", "col"))
    ends = jnp.cumsum(lengths)
    starts = ends - lengths
    positions = ex_index * tokens + jnp.arange(tokens, dtype=jnp.int32)
    member = (
        (positions[None, :] >= starts[:, None]) & (positions[None, :] < ends[:, None])
    ).astype(jnp.float32)
    local_part = lax.dot_general(token_scores, member, (((1,), (1,)), ((), ())), precision=highest)
    example_scores = lax.psum(local_part, "ex")
    return (token_scores, example_scores)


def solution(mesh):
    placed = (
        P("ex", "row"),
        P("ex", "col"),
        P("ex", "row"),
        P("ex", "col"),
        P("ex"),
        P("row", None, None),
        P("col", None, None),
        P(),
        P("row"),
        P("col"),
        P(),
    )
    return jax.shard_map(
        body, mesh=mesh, in_specs=placed, out_specs=(P(None, "ex"), P()), check_vma=False
    )
```

profile of v0, /device:TPU:0, one launch (start us, length us, event | category | flops | bytes accessed | tf_op | source)
XLA Modules:
  0.0 449.4 jit_solution(11609939477935120614)
XLA Ops:
  8.0 5.9 %fusion.58 = (bf16[4,512,1024]{2,1,0:T(8,128)(2,1)}, bf16[4,512,1024]{2,1,0:T(8,128)(2,1)}) fusion(bf16[4,1024,1024]{2,1,0:T(8,128)(2,1)} %param.19), kind=kLoop, calls=%fused_computation.93 | loop fusion | bytes 16777216 | tf_op jit(solution)/shard_map/jit(_take)/gather | solution.py:38
  14.0 5.0 %gather_fusion.4 = bf16[4,512,1024]{2,1,0:T(8,128)(2,1)} fusion(bf16[4,512,1024]{2,1,0:T(8,128)(2,1)} %get-tuple-element.229, s32[1024]{0:T(1024)S(1)} %pad_clamp_fusion.1), kind=kCustom, calls=%fused_computation.4 | custom fusion | bytes 8388624 | tf_op jit(solution)/shard_map/jit(_take)/gather | solution.py:38
  19.0 5.1 %gather_fusion.5 = bf16[4,512,1024]{2,1,0:T(8,128)(2,1)} fusion(bf16[4,512,1024]{2,1,0:T(8,128)(2,1)} %get-tuple-element.230, s32[1024]{0:T(1024)S(1)} %pad_clamp_fusion.1), kind=kCustom, calls=%fused_computation.5 | custom fusion | bytes 8388624 | tf_op jit(solution)/shard_map/jit(_take)/gather | solution.py:38
  24.1 8.5 %all_gather.14 = bf16[128,2048]{1,0:T(8,128)(2,1)S(1)} all-gather(bf16[32,2048]{1,0:T(8,128)(2,1)S(1)} %copy-done.4), channel_id=1, replica_groups=mesh['row'=4,'col'=2,'ex'=4] {'ex'}, dimensions={0}, use_global_device_ids=true | all-gather | bytes 655360 | tf_op jit(solution)/shard_map/all_gather | solution.py:41
  34.6 6.7 %all-reduce = bf16[128]{0:T(256)(128)(2,1)S(1)} all-reduce(bf16[128]{0:T(256)(128)(2,1)S(1)} %dynamic-update-slice), channel_id=1, replica_groups=mesh['row'=4,'col'=2,'ex'=4] {'ex'}, use_global_device_ids=true, to_apply=%add | all-reduce | flops 128 | bytes 512
  41.9 4.2 fusion.59
  46.1 4.4 gather_fusion.6
  50.4 2.7 gather_fusion.7
  54.6 1.6 fusion.34
  56.3 1.6 copy.27
  59.0 15.5 %fusion.15 = bf16[4,1024,1024]{2,1,0:T(8,128)(2,1)} fusion(bf16[4,128,1024]{2,1,0:T(8,128)(2,1)S(1)} %gather_fusion.1, bf16[4,128,1024]{2,1,0:T(8,128)(2,1)S(1)} %gather_fusion, pred[4]{0:T(512)(128)(4,1)S(1)} %compare_and_fusion.2, pred[4]{0:T(512)(128)(4,1)S(1)} %compare_and_fusion.3, bf16[128,4]{0,1:T(4,128)(2,1)S(1)} %compare_convert_fusion.1, ...), kind=kOutput, calls=%fused_computation.27 | convolution fusion | flops 9690415104 | bytes 18875400 | tf_op jit(solution)/shard_map/kab,kac->kbc/dot_general | solution.py:51
  74.6 17.2 %fusion.13 = f32[4,1024,1024]{2,1,0:T(8,128)} fusion(bf16[4,1024,1024]{2,1,0:T(8,128)(2,1)} %fusion.15, bf16[4,512,1024]{2,1,0:T(8,128)(2,1)} %gather_fusion.7, bf16[4,512,1024]{2,1,0:T(8,128)(2,1)} %gather_fusion.6, pred[4]{0:T(512)(128)(4,1)S(1)} %compare_and_fusion.2), kind=kOutput, calls=%fused_computation.25 | convolution fusion | flops 8610906112 | bytes 33554436 | tf_op jit(solution)/shard_map/kbc,kcd->kbd/dot_general | solution.py:54
  91.7 13.6 %divide_convert_fusion = bf16[4,1024,1024]{2,1,0:T(8,128)(2,1)} fusion(f32[4,1024,1024]{2,1,0:T(8,128)} %fusion.13, f32[4,1024,64]{1,2,0:T(8,128)S(1)} %copy-done.3, s32[4,1024]{1,0:T(4,128)S(1)} %broadcast_select_fusion), kind=kOutput, calls=%fused_computation.20 | convolution fusion | flops 3234070528 | bytes 26230784 | tf_op jit(solution)/shard_map/kbm,kdm->kbd/dot_general | solution.py:61
  105.3 22.7 %fusion.17 = bf16[4,1024,1024]{2,1,0:T(8,128)(2,1)} fusion(bf16[4,1024,1024]{2,1,0:T(8,128)(2,1)} %divide_convert_fusion, bf16[4,512,1024]{2,1,0:T(8,128)(2,1)} %gather_fusion.7, bf16[4,512,1024]{2,1,0:T(8,128)(2,1)} %gather_fusion.6, pred[4]{0:T(512)(128)(4,1)S(1)} %compare_and_fusion.2, bf16[4,512,1024]{2,1,0:T(8,128)(2,1)} %gather_fusion.5, ...), kind=kOutput, calls=%fused_computation.29 | convolution fusion | flops 17230200832 | bytes 33554440 | tf_op jit(solution)/shard_map/kab,kbc->kac/dot_general | solution.py:66
  128.0 6.6 %copy.34 = bf16[512,4096]{0,1:T(8,128)(2,1)} copy(bf16[512,4096]{1,0:T(8,128)(2,1)} %param.14) | data formatting | bytes 8388608 | tf_op args[1]
  134.6 2.5 copy.26
  137.3 193.0 %all-gather.5.cloned.1.call-done = bf16[16,1024,1024]{2,1,0:T(8,128)(2,1)} async-done(((bf16[4,1024,1024]{2,1,0:T(8,128)(2,1)}), bf16[16,1024,1024]{2,1,0:T(8,128)(2,1)}) %all-gather.5.cloned.1.call-update) | async-done | bytes 33554448 | tf_op jit(solution)/shard_map/all_gather | solution.py:73
  330.4 84.1 %while.17 = (s32[]{:T(128)}, f32[2,512]{1,0:T(2,128)S(1)}, bf16[512,2,1024]{0,2,1:T(8,128)(2,1)}, bf16[16,1024,1024]{2,1,0:T(8,128)(2,1)}, bf16[512,4,1024]{0,2,...) while((s32[]{:T(128)}, f32[2,512]{1,0:T(2,128)S(1)}, ...), condition=%wide.region_2.3_spmd.clone, body=%wide.region_0.2_spmd.clone.sunk | while | flops 1075317248 | bytes 8401917 | solution.py:87
  332.2 3.3 fusion.69
  335.6 1.3 constant_dynamic-slice_fusion.2
  337.5 3.3 fusion.69
  340.9 1.3 constant_dynamic-slice_fusion.2
  342.7 3.3 fusion.69
  346.1 1.3 constant_dynamic-slice_fusion.2
  348.0 3.3 fusion.69
  351.4 1.3 constant_dynamic-slice_fusion.2
  353.2 3.3 fusion.69
  358.5 3.3 fusion.69
  361.9 1.3 constant_dynamic-slice_fusion.2
  363.8 3.3 fusion.69
  367.2 1.3 constant_dynamic-slice_fusion.2
  369.0 3.3 fusion.69
  372.4 1.3 constant_dynamic-slice_fusion.2
  374.3 3.3 fusion.69
  377.7 1.3 constant_dynamic-slice_fusion.2
  379.5 3.3 fusion.69
  384.8 3.3 fusion.69
  390.0 3.3 fusion.69
  393.4 1.3 constant_dynamic-slice_fusion.2
  395.3 3.3 fusion.69
  398.7 1.3 constant_dynamic-slice_fusion.2
  400.5 3.3 fusion.69
  403.9 1.3 constant_dynamic-slice_fusion.2
  405.8 3.3 fusion.69
  409.2 1.3 constant_dynamic-slice_fusion.2
  411.0 3.3 fusion.69
  414.4 21.5 %psum.14 = f32[2,512]{1,0:T(2,128)S(1)} all-reduce(f32[2,512]{1,0:T(2,128)S(1)} %get-tuple-element.183), channel_id=1, replica_groups=mesh['row'=4,'col'=2,'ex'=4] {'row','col'}, use_global_device_ids=true, to_apply=%region_3.4 | all-reduce | flops 1024 | bytes 8192 | tf_op jit(solution)/shard_map/psum | solution.py:90
  436.1 6.5 %psum.15 = f32[2,4]{1,0:T(2,128)} all-reduce(f32[2,4]{1,0:T(2,128)S(1)} %fusion.42), channel_id=1, replica_groups=mesh['row'=4,'col'=2,'ex'=4] {'ex'}, use_global_device_ids=true, to_apply=%region_5.6 | all-reduce | flops 8 | bytes 64 | tf_op jit(solution)/shard_map/psum | solution.py:98
  (108 shorter events, 20.9 us)
Async XLA Ops:
  7.2 47.5 %copy-start = (f32[64,64]{1,0:T(8,128)S(1)}, f32[64,64]{1,0:T(8,128)}, u32[]{:S(2)}) copy-start(f32[64,64]{1,0:T(8,128)} %param.20) | copy-start | bytes 49156
  7.2 49.1 %all-gather.3.cloned.1.call-start = ((), (), s32[]{:S(2)}) async-start(), calls=%async_computation | async-start | bytes 1310720 | tf_op jit(solution)/shard_map/all_gather | solution.py:42
  7.9 322.5 %all-gather.5.cloned.1.call-start = ((), (), s32[]{:S(2)}) async-start(), calls=%async_computation.1 | async-start | bytes 41943040 | tf_op jit(solution)/shard_map/all_gather | solution.py:73
  13.9 10.1 %copy-start.4 = (bf16[32,2048]{1,0:T(8,128)(2,1)S(1)}, bf16[32,2048]{1,0:T(8,128)(2,1)}, u32[]{:S(2)}) copy-start(bf16[32,2048]{1,0:T(8,128)(2,1)} %param.15) | copy-start | bytes 393220
  14.0 19.1 %copy-start.8 = (s32[32]{0:T(128)S(1)}, s32[32]{0:T(128)}, u32[]{:S(2)}) copy-start(s32[32]{0:T(128)} %param.17) | copy-start | bytes 388
  14.0 19.1 %copy-start.10 = (u32[32]{0:T(128)S(1)}, u32[32]{0:T(128)}, u32[]{:S(2)}) copy-start(u32[32]{0:T(128)} %constant.274) | copy-start | bytes 388
  46.1 7.1 %copy-start.6 = (s32[2048]{0:T(1024)S(1)}, s32[2048]{0:T(1024)}, u32[]{:S(2)}) copy-start(s32[2048]{0:T(1024)} %param.21) | copy-start | bytes 24580
  46.1 7.7 %copy-start.5 = (s32[4096]{0:T(1024)S(1)}, s32[4096]{0:T(1024)}, u32[]{:S(2)}) copy-start(s32[4096]{0:T(1024)} %param.22) | copy-start | bytes 49156
  74.6 17.2 %copy-start.3 = (f32[4,1024,64]{1,2,0:T(8,128)S(1)}, f32[4,1024,64]{1,2,0:T(8,128)}, u32[]{:S(2)}) copy-start(f32[4,1024,64]{1,2,0:T(8,128)} %fusion.34) | copy-start | bytes 3145732
  128.0 6.6 %copy-start.2 = (bf16[512,2048]{1,0:T(8,128)(2,1)S(1)}, bf16[512,2048]{1,0:T(8,128)(2,1)}, u32[]{:S(2)}) copy-start(bf16[512,2048]{1,0:T(8,128)(2,1)} %param.13) | copy-start | bytes 6291460
  128.0 9.1 %copy-start.9 = (s32[4]{0:T(128)S(1)}, s32[4]{0:T(128)}, u32[]{:S(2)}) copy-start(s32[4]{0:T(128)} %param.23) | copy-start | bytes 52
  414.4 28.2 %copy-start.1 = (f32[64,64]{1,0:T(8,128)S(1)}, f32[64,64]{1,0:T(8,128)}, u32[]{:S(2)}) copy-start(f32[64,64]{1,0:T(8,128)} %param.20) | copy-start | bytes 49156
  435.9 6.7 %copy-start.7 = (f32[2,512]{1,0:T(2,128)}, f32[2,512]{1,0:T(2,128)S(1)}, u32[]{:S(2)}) copy-start(f32[2,512]{1,0:T(2,128)S(1)} %psum.14) | copy-start | bytes 12292
Sparse Core Ops, SparseCore 0:
  9.5 19.4 all-gather.2
  128.1 202.1 all-gather.4
where the time goes:
time: 451 us; the launch traced here: 449 us
  waiting for transfers between devices  194 us (43%)
  matrix products  124 us (27%)
  local copies, waits for them, and re-layouts  71.6 us (16%)
  blocking collectives  43.1 us (10%)
  between operations  14.9 us (3%)
    all_gather x1, waiting for transfers between devices, body(): piece = lax.all_gather(precond, 'ex', axis=0, tiled=True)  193 us
    dot_general x16, matrix products, score_one(): lax.dot_general(acts, matrix, (((1,), (1,)), ((), ())), preferred_element...  52.8 us
    dynamic_slice x32, local copies, waits for them, and re-layouts, score_one(): lax.dynamic_index_in_dim(out_split, pair // in_sub, 1, keepdims=False)  29.2 us
    dot_general x1, matrix products, body(): jnp.einsum('kab,kbc->kac', out_own, back, preferred_element_type=jnp.floa...  22.7 us
    psum x1, blocking collectives, body(): token_scores = lax.psum(token_part, ('row', 'col'))  21.5 us
    dot_general x1, matrix products, body(): jnp.einsum('kbc,kcd->kbd', half, in_own, preferred_element_type=jnp.float32)  17.2 us
    gather x3, local copies, waits for them, and re-layouts, body(): out_own = jnp.take(out_basis, out_of, axis=0)  16 us
    dot_general x1, matrix products, body(): jnp.einsum('kab,kac->kbc', out_own, grad_own, preferred_element_type=jnp....  15.5 us
  transfers between devices with their start and end apart: 2, of which 1 were waited for; matrix products, arithmetic and copies ran while one was open for 9% of the time, Pallas kernels for 0%

commit v1 on v0

v1 whole, which is shorter than its diff:
```python
import functools

import jax
import jax.numpy as jnp
from jax import lax
from jax.experimental import pallas as pl
from jax.experimental.pallas import tpu as pltpu
from jax.sharding import PartitionSpec as P

QUERIES = 2
DAMPING = 0.1
MESH = pl.DeviceIdType.MESH
F32 = jnp.float32
BF16 = jnp.bfloat16


def dot(a, b):
    return jnp.dot(a, b, preferred_element_type=F32)


def kernel(
    sizes,
    train_in,
    train_out,
    query_in,
    query_out,
    ids,
    in_basis,
    out_basis,
    table_ref,
    in_level,
    out_level,
    lengths,
    token_out,
    example_out,
    acts,
    grads,
    basis_in,
    basis_out,
    q_in,
    q_out,
    q_ids,
    hot_t,
    inverse,
    left,
    right,
    damp0,
    damp1,
    acc0,
    acc1,
    lanes,
    parts,
    sums,
    load_sem,
    q_load_sem,
    q_send_sem,
    q_fwd_sem,
    q_recv_sem,
    part_send,
    part_recv,
    sum_send,
    sum_recv,
):
    rows, cols, exs, tile = sizes
    row, col, ex = lax.axis_index("row"), lax.axis_index("col"), lax.axis_index("ex")
    in_sub, width, _ = in_basis.shape
    out_sub = out_basis.shape[0]
    tokens = train_in.shape[0]
    held = query_in.shape[0]
    group = rows * cols
    place = row * cols + col
    chips = exs // 2
    sibling = ex + 1 - 2 * lax.rem(ex, 2)

    def ex_peer(k):
        return lax.rem(ex + k, exs)

    def group_peer(k):
        other = lax.rem(place + k, group)
        return {"row": other // cols, "col": lax.rem(other, cols)}

    def slot(ref, e):
        return ref.at[pl.ds(pl.multiple_of(e * held, held), held), :]

    own = [
        pltpu.make_async_copy(src, slot(ref, ex), q_load_sem.at[n])
        for n, (src, ref) in enumerate(((ids, q_ids), (query_in, q_in), (query_out, q_out)))
    ]
    for copy in own:
        copy.start()
    in_loads, out_loads = [], []
    for j in range(in_sub):
        in_loads.append(
            (
                pltpu.make_async_copy(
                    train_in.at[:, pl.ds(j * width, width)], acts.at[j], load_sem.at[0, 0, j]
                ),
                pltpu.make_async_copy(in_basis.at[j], basis_in.at[j], load_sem.at[0, 1, j]),
            )
        )
    for i in range(out_sub):
        out_loads.append(
            (
                pltpu.make_async_copy(
                    train_out.at[:, pl.ds(i * width, width)], grads.at[i], load_sem.at[1, 0, i]
                ),
                pltpu.make_async_copy(out_basis.at[i], basis_out.at[i], load_sem.at[1, 1, i]),
            )
        )
    for pair in in_loads + out_loads:
        for copy in pair:
            copy.start()

    barrier = pltpu.get_barrier_semaphore()
    for k in range(1, exs):
        pl.semaphore_signal(barrier, inc=1, device_id={"ex": ex_peer(k)}, device_id_type=MESH)
    for k in range(1, group):
        pl.semaphore_signal(barrier, inc=1, device_id=group_peer(k), device_id_type=MESH)
    pl.semaphore_wait(barrier, exs - 1 + group - 1)

    gathered = (q_ids, q_in, q_out)

    def move(n, e, to, send):
        return pltpu.make_async_remote_copy(
            src_ref=slot(gathered[n], e),
            dst_ref=slot(gathered[n], e),
            send_sem=send,
            recv_sem=q_recv_sem.at[n, e],
            device_id={"ex": to},
            device_id_type=MESH,
        )

    firsts = []
    for n in range(3):
        own[n].wait()
        for k in range(1, chips):
            firsts.append(move(n, ex, ex_peer(2 * k), q_send_sem.at[n, k]))
        firsts.append(move(n, ex, sibling, q_send_sem.at[n, 0]))
    for copy in firsts:
        copy.start()

    for j in range(in_sub):
        for copy in in_loads[j]:
            copy.wait()
        acts[j] = dot(acts[j], basis_in[j]).astype(BF16)
    for i in range(out_sub):
        for copy in out_loads[i]:
            copy.wait()
        grads[i] = dot(grads[i], basis_out[i]).astype(BF16)

    forwards = []
    for n in range(3):
        for k in range(1, chips):
            source = lax.rem(ex + exs - 2 * k, exs)
            move(n, source, sibling, q_fwd_sem.at[n, k]).wait_recv()
            forwards.append(move(n, source, sibling, q_fwd_sem.at[n, k]))
            forwards[-1].start()

    table = 1.0 / (table_ref[...] + DAMPING)
    levels = table.shape[0]
    high = table.astype(BF16)
    low = (table - high.astype(F32)).astype(BF16)
    split = jnp.concatenate([high.astype(F32), low.astype(F32)], axis=0).astype(BF16)
    n_in, n_out = in_sub * width, out_sub * width
    in_hot = (
        lax.broadcasted_iota(jnp.int32, (levels, n_in), 0) == in_level[...]
    ).astype(F32).astype(BF16)
    spread = dot(split, in_hot).astype(BF16)
    for i in range(out_sub):
        out_hot = (
            lax.rem(lax.broadcasted_iota(jnp.int32, (2 * levels, width), 0), levels)
            == out_level[:, pl.ds(i * width, width)]
        ).astype(F32)
        hot_t[pl.ds(i * width, width), :] = out_hot.T.astype(BF16)
    step = width // 4

    def expand(k, carry):
        at = pl.ds(pl.multiple_of(k * step, step), step)
        inverse[at, :] = dot(hot_t[at, :], spread).astype(BF16)
        return carry

    lax.fori_loop(0, n_out // step, expand, 0)

    for n in range(3):
        move(n, sibling, sibling, q_send_sem.at[n, 0]).wait_recv()
        for k in range(1, chips):
            source = lax.rem(sibling + exs - 2 * k, exs)
            move(n, source, sibling, q_send_sem.at[n, 0]).wait_recv()
    for copy in firsts + forwards:
        copy.wait_send()

    count = exs * held
    who = q_ids[:, 0:1]
    for j in range(in_sub):
        turned = dot(q_in[:, pl.ds(j * width, width)], basis_in[j])
        for q in range(QUERIES):
            right[q, :, pl.ds(j * width, width)] = jnp.where(who == q, turned, 0.0).astype(BF16)
    for i in range(out_sub):
        turned = dot(q_out[:, pl.ds(i * width, width)], basis_out[i])
        left[pl.ds(i * width, width), :] = turned.T.astype(BF16)

    damps, accs = (damp0, damp1), (acc0, acc1)
    lanes[...] = jnp.zeros_like(lanes)
    tiles = n_in // tile
    per = width // tile

    def build(q, n):
        c, i = n // out_sub, lax.rem(n, out_sub)
        at_c = pl.ds(pl.multiple_of(c * tile, tile), tile)
        at_r = pl.ds(pl.multiple_of(i * width, width), width)
        rotated = dot(left[at_r, :], right[q, :, at_c])
        damps[q][...] = (rotated * inverse[at_r, at_c].astype(F32)).astype(BF16)

    def outer(c, carry):
        for q in range(QUERIES):
            accs[q][...] = jnp.zeros_like(accs[q])

        def inner(i, carry):
            n = c * out_sub + i
            build(1, n)
            accs[0][...] += dot(grads[i], damp0[...])
            build(0, jnp.minimum(n + 1, tiles * out_sub - 1))
            accs[1][...] += dot(grads[i], damp1[...])
            return carry

        lax.fori_loop(0, out_sub, inner, 0)
        x = acts[c // per, :, pl.ds(pl.multiple_of(lax.rem(c, per) * tile, tile), tile)].astype(F32)
        for q in range(QUERIES):
            product = accs[q][...] * x
            total = product[:, 0:128]
            for g in range(1, tile // 128):
                total = total + product[:, g * 128 : (g + 1) * 128]
            lanes[q] += total
        return carry

    build(0, 0)
    lax.fori_loop(0, tiles, outer, 0)

    mine = jnp.concatenate(
        [jnp.sum(lanes[q].T, axis=0, keepdims=True) for q in range(QUERIES)], axis=0
    )
    parts[place] = mine
    sends = []
    for k in range(1, group):
        sends.append(
            pltpu.make_async_remote_copy(
                src_ref=parts.at[place],
                dst_ref=parts.at[place],
                send_sem=part_send.at[k],
                recv_sem=part_recv.at[place],
                device_id=group_peer(k),
                device_id_type=MESH,
            )
        )
        sends[-1].start()
    for k in range(1, group):
        source = lax.rem(place + k, group)
        pltpu.make_async_remote_copy(
            src_ref=parts.at[source],
            dst_ref=parts.at[source],
            send_sem=part_send.at[k],
            recv_sem=part_recv.at[source],
            device_id=group_peer(k),
            device_id_type=MESH,
        ).wait_recv()
    for copy in sends:
        copy.wait_send()
    scores = jnp.sum(parts[...], axis=0)
    token_out[...] = scores

    position = ex * tokens + lax.broadcasted_iota(jnp.int32, (QUERIES, tokens), 1)
    lane = lax.broadcasted_iota(jnp.int32, (QUERIES, 128), 1)
    found = jnp.zeros((QUERIES, 128), F32)
    start = jnp.int32(0)
    for e in range(lengths.shape[0]):
        end = start + lengths[e]
        inside = (position >= start) & (position < end)
        value = jnp.sum(jnp.where(inside, scores, 0.0), axis=1, keepdims=True)
        found = jnp.where(lane == e, value, found)
        start = end
    sums[ex] = found
    sends = []
    for k in range(1, exs):
        sends.append(
            pltpu.make_async_remote_copy(
                src_ref=sums.at[ex],
                dst_ref=sums.at[ex],
                send_sem=sum_send.at[k],
                recv_sem=sum_recv.at[ex],
                device_id={"ex": ex_peer(k)},
                device_id_type=MESH,
            )
        )
        sends[-1].start()
    for k in range(1, exs):
        source = ex_peer(k)
        pltpu.make_async_remote_copy(
            src_ref=sums.at[source],
            dst_ref=sums.at[source],
            send_sem=sum_send.at[k],
            recv_sem=sum_recv.at[source],
            device_id={"ex": source},
            device_id_type=MESH,
        ).wait_recv()
    for copy in sends:
        copy.wait_send()
    example_out[...] = jnp.sum(sums[...], axis=0)[:, 0 : lengths.shape[0]]


def solution(mesh):
    rows, cols, exs = mesh.shape["row"], mesh.shape["col"], mesh.shape["ex"]

    def body(
        train_in,
        train_out,
        query_in,
        query_out,
        query_ids,
        in_basis,
        out_basis,
        level_table,
        in_level,
        out_level,
        lengths,
    ):
        in_sub, width, _ = in_basis.shape
        out_sub = out_basis.shape[0]
        tokens, held = train_in.shape[0], query_in.shape[0]
        count = exs * held
        n_in, n_out = in_sub * width, out_sub * width
        levels = level_table.shape[0]
        tile = width // 2
        group = rows * cols
        ids = jnp.broadcast_to(query_ids[:, None], (held, 128))
        hbm = pl.BlockSpec(memory_space=pl.ANY)
        vmem = pl.BlockSpec(memory_space=pltpu.VMEM)
        smem = pl.BlockSpec(memory_space=pltpu.SMEM)
        most = max(in_sub, out_sub)
        dma = pltpu.SemaphoreType.DMA
        return pl.pallas_call(
            functools.partial(kernel, (rows, cols, exs, tile)),
            out_shape=(
                jax.ShapeDtypeStruct((QUERIES, tokens), F32),
                jax.ShapeDtypeStruct((QUERIES, lengths.shape[0]), F32),
            ),
            in_specs=[hbm] * 7 + [vmem] * 3 + [smem],
            out_specs=(vmem, vmem),
            scratch_shapes=[
                pltpu.VMEM((in_sub, tokens, width), BF16),
                pltpu.VMEM((out_sub, tokens, width), BF16),
                pltpu.VMEM((in_sub, width, width), BF16),
                pltpu.VMEM((out_sub, width, width), BF16),
                pltpu.VMEM((count, n_in), BF16),
                pltpu.VMEM((count, n_out), BF16),
                pltpu.VMEM((count, 128), jnp.int32),
                pltpu.VMEM((n_out, 2 * levels), BF16),
                pltpu.VMEM((n_out, n_in), BF16),
                pltpu.VMEM((n_out, count), BF16),
                pltpu.VMEM((QUERIES, count, n_in), BF16),
                pltpu.VMEM((width, tile), BF16),
                pltpu.VMEM((width, tile), BF16),
                pltpu.VMEM((tokens, tile), F32),
                pltpu.VMEM((tokens, tile), F32),
                pltpu.VMEM((QUERIES, tokens, 128), F32),
                pltpu.VMEM((group, QUERIES, tokens), F32),
                pltpu.VMEM((exs, QUERIES, 128), F32),
                dma((2, 2, most)),
                dma((3,)),
                dma((3, exs // 2)),
                dma((3, exs // 2)),
                dma((3, exs)),
                dma((group,)),
                dma((group,)),
                dma((exs,)),
                dma((exs,)),
            ],
            compiler_params=pltpu.CompilerParams(
                collective_id=0, has_side_effects=True, vmem_limit_bytes=66 * 1000 * 1000
            ),
        )(
            train_in,
            train_out,
            query_in,
            query_out,
            ids,
            in_basis,
            out_basis,
            level_table,
            in_level[None, :],
            out_level[None, :],
            lengths,
        )

    placed = (
        P("ex", "row"),
        P("ex", "col"),
        P("ex", "row"),
        P("ex", "col"),
        P("ex"),
        P("row", None, None),
        P("col", None, None),
        P(),
        P("row"),
        P("col"),
        P(),
    )
    return jax.shard_map(
        body, mesh=mesh, in_specs=placed, out_specs=(P(None, "ex"), P()), check_vma=False
    )
```

time: 451 us -> 73 us (0.16)
  waiting for transfers between devices: 194 us -> 0 us
  matrix products: 124 us -> 0 us
  Pallas kernels: 0 us -> 68.3 us
  local copies, waits for them, and re-layouts: 71.6 us -> 3.82 us
  blocking collectives: 43.1 us -> 0 us
  between operations: 14.9 us -> 0.64 us
    all_gather x2 -> x0, waiting for transfers between devices: 193 us -> none  [the longest x1 193 us: body(): piece = lax.all_gather(precond, 'ex', axis=0, tiled=True)]
    dot_general x22 -> x0, matrix products: 124 us -> none  [the longest x16 52.8 us: score_one(): lax.dot_general(acts, matrix, (((1,), (1,)), ((), ())), preferred_element...]
    pallas_call x0 -> x1, Pallas kernels: none -> 68.3 us  [body(): pl.pallas_call(functools.partial(kernel, (rows, cols, exs, tile)), out_sh...]
    gather x10 -> x0, local copies, waits for them, and re-layouts: 29.7 us -> none  [the longest x3 16 us: body(): out_own = jnp.take(out_basis, out_of, axis=0)]
    dynamic_slice x32 -> x0, local copies, waits for them, and re-layouts: 29.2 us -> none  [score_one(): lax.dynamic_index_in_dim(out_split, pair // in_sub, 1, keepdims=False)]
    psum x2 -> x0, blocking collectives: 27.9 us -> none  [the longest x1 21.5 us: body(): token_scores = lax.psum(token_part, ('row', 'col'))]
    all_gather x1 -> x0, blocking collectives: 8.47 us -> none  [body(): piece_in = lax.all_gather(query_in, 'ex', axis=0, tiled=True)]
    unnamed x27 -> x2, local copies, waits for them, and re-layouts: 9.99 us -> 2.49 us
  transfers between devices with their start and end apart: 2 -> 0, of which waited for: 1 -> 0; matrix products, arithmetic and copies ran while one was open for 9% -> 0% of each run, Pallas kernels for 0% -> 0%
where the time goes in v1:
time: 73 us; the launch traced here: 72.7 us
  Pallas kernels  68.3 us (94%)
  local copies, waits for them, and re-layouts  3.82 us (5%)
    pallas_call x1, Pallas kernels, body(): pl.pallas_call(functools.partial(kernel, (rows, cols, exs, tile)), out_sh...  68.3 us
    unnamed x2, local copies, waits for them, and re-layouts  2.49 us

profile of v1, /device:TPU:0, one launch (start us, length us, event | category | flops | bytes accessed | tf_op | source)
XLA Modules:
  0.0 72.7 jit_solution(12145591693177176623)
XLA Ops:
  0.6 1.3 %broadcast_in_dim.12.ids = s32[32,128]{1,0:T(8,128)} broadcast(s32[32]{0:T(128)} %param.15), dimensions={0} | broadcast | bytes 16512 | tf_op jit(solution)/shard_map/broadcast_in_dim | solution.py:334
  2.0 68.3 %shard_map.122 = (f32[2,512]{1,0:T(2,128)}, f32[2,4]{1,0:T(2,128)}) custom-call(bf16[512,2048]{1,0:T(8,128)(2,1)} %train_in.1, bf16[512,4096]{1,0:T(8,128)(2,1)} %train_out.1, bf16[32,2048]{1,0:T(8,128)(2,1)} %query_in.1, bf16[32,4096]{1,0:T(8,128)(2,1)} %query_out.1, s32[32,128]{1,0:T(8,128)} %broadcast_in_dim.12.ids, bf16[2,1024,1024]{2,1,0:T(8,128)(2,1)} %in_basis.1, ...), custom_call_target="tpu_custom_call" | custom-call | tf_op jit(solution)/shard_map/pallas_call | solution.py:340
  70.2 1.3 %copy.15 = f32[2,512]{1,0:T(2,128)} copy(f32[2,512]{1,0:T(2,128)} %get-tuple-element.4) | data formatting | bytes 8192
  71.5 1.2 %copy.16 = f32[2,4]{1,0:T(2,128)} copy(f32[2,4]{1,0:T(2,128)} %get-tuple-element.5) | data formatting | bytes 64

commit v2 on v1

--- a/solution.py
+++ b/solution.py
@@ -46,8 +46,6 @@
     right,
     damp0,
     damp1,
-    acc0,
-    acc1,
     lanes,
     parts,
     sums,
@@ -84,7 +82,7 @@
 
     own = [
         pltpu.make_async_copy(src, slot(ref, ex), q_load_sem.at[n])
-        for n, (src, ref) in enumerate(((ids, q_ids), (query_in, q_in), (query_out, q_out)))
+        for n, (src, ref) in enumerate(((query_in, q_in), (query_out, q_out)))
     ]
     for copy in own:
         copy.start()
@@ -102,7 +100,7 @@
         out_loads.append(
             (
                 pltpu.make_async_copy(
-                    train_out.at[:, pl.ds(i * width, width)], grads.at[i], load_sem.at[1, 0, i]
+                    train_out.at[:, pl.ds(i * width, width)], grads.at[:, pl.ds(i * width, width)], load_sem.at[1, 0, i]
                 ),
                 pltpu.make_async_copy(out_basis.at[i], basis_out.at[i], load_sem.at[1, 1, i]),
             )
@@ -110,6 +108,12 @@
     for pair in in_loads + out_loads:
         for copy in pair:
             copy.start()
+
+    at_row = lax.broadcasted_iota(jnp.int32, (held, 128), 0)
+    code = jnp.zeros((held, 128), jnp.int32)
+    for t in range(held):
+        code = jnp.where(at_row == t, ids[t], code)
+    q_ids[pl.ds(pl.multiple_of(ex * held, held), held), :] = code
 
     barrier = pltpu.get_barrier_semaphore()
     for k in range(1, exs):
@@ -118,7 +122,7 @@
         pl.semaphore_signal(barrier, inc=1, device_id=group_peer(k), device_id_type=MESH)
     pl.semaphore_wait(barrier, exs - 1 + group - 1)
 
-    gathered = (q_ids, q_in, q_out)
+    gathered = (q_in, q_out, q_ids)
 
     def move(n, e, to, send):
         return pltpu.make_async_remote_copy(
@@ -132,12 +136,13 @@
 
     firsts = []
     for n in range(3):
-        own[n].wait()
+        if n < len(own):
+            own[n].wait()
         for k in range(1, chips):
             firsts.append(move(n, ex, ex_peer(2 * k), q_send_sem.at[n, k]))
         firsts.append(move(n, ex, sibling, q_send_sem.at[n, 0]))
-    for copy in firsts:
-        copy.start()
+        for copy in firsts[-chips:]:
+            copy.start()
 
     for j in range(in_sub):
         for copy in in_loads[j]:
@@ -146,15 +151,8 @@
     for i in range(out_sub):
         for copy in out_loads[i]:
             copy.wait()
-        grads[i] = dot(grads[i], basis_out[i]).astype(BF16)
-
-    forwards = []
-    for n in range(3):
-        for k in range(1, chips):
-            source = lax.rem(ex + exs - 2 * k, exs)
-            move(n, source, sibling, q_fwd_sem.at[n, k]).wait_recv()
-            forwards.append(move(n, source, sibling, q_fwd_sem.at[n, k]))
-            forwards[-1].start()
+        at = pl.ds(i * width, width)
+        grads[:, at] = dot(grads[:, at], basis_out[i]).astype(BF16)
 
     table = 1.0 / (table_ref[...] + DAMPING)
     levels = table.shape[0]
@@ -179,15 +177,25 @@
         inverse[at, :] = dot(hot_t[at, :], spread).astype(BF16)
         return carry
 
-    lax.fori_loop(0, n_out // step, expand, 0)
+    whole = n_out // step
+    first = whole * 5 // 8
+    lax.fori_loop(0, first, expand, 0)
+
+    forwards = []
+    for n in range(3):
+        for k in range(1, chips):
+            source = lax.rem(ex + exs - 2 * k, exs)
+            move(n, source, sibling, q_fwd_sem.at[n, k]).wait_recv()
+            forwards.append(move(n, source, sibling, q_fwd_sem.at[n, k]))
+            forwards[-1].start()
+
+    lax.fori_loop(first, whole, expand, 0)
 
     for n in range(3):
         move(n, sibling, sibling, q_send_sem.at[n, 0]).wait_recv()
         for k in range(1, chips):
             source = lax.rem(sibling + exs - 2 * k, exs)
             move(n, source, sibling, q_send_sem.at[n, 0]).wait_recv()
-    for copy in firsts + forwards:
-        copy.wait_send()
 
     count = exs * held
     who = q_ids[:, 0:1]
@@ -199,38 +207,31 @@
         turned = dot(q_out[:, pl.ds(i * width, width)], basis_out[i])
         left[pl.ds(i * width, width), :] = turned.T.astype(BF16)
 
-    damps, accs = (damp0, damp1), (acc0, acc1)
+    damps = (damp0, damp1)
     lanes[...] = jnp.zeros_like(lanes)
     tiles = n_in // tile
     per = width // tile
 
-    def build(q, n):
-        c, i = n // out_sub, lax.rem(n, out_sub)
+    def build(q, c):
         at_c = pl.ds(pl.multiple_of(c * tile, tile), tile)
-        at_r = pl.ds(pl.multiple_of(i * width, width), width)
-        rotated = dot(left[at_r, :], right[q, :, at_c])
-        damps[q][...] = (rotated * inverse[at_r, at_c].astype(F32)).astype(BF16)
+        for i in range(out_sub):
+            at_r = pl.ds(i * width, width)
+            rotated = dot(left[at_r, :], right[q, :, at_c])
+            damps[q][at_r, :] = (rotated * inverse[at_r, at_c].astype(F32)).astype(BF16)
+
+    def score(q, c):
+        x = acts[c // per, :, pl.ds(pl.multiple_of(lax.rem(c, per) * tile, tile), tile)]
+        product = dot(grads[...], damps[q][...]) * x.astype(F32)
+        total = product[:, 0:128]
+        for g in range(1, tile // 128):
+            total = total + product[:, g * 128 : (g + 1) * 128]
+        lanes[q] += total
 
     def outer(c, carry):
-        for q in range(QUERIES):
-            accs[q][...] = jnp.zeros_like(accs[q])
-
-        def inner(i, carry):
-            n = c * out_sub + i
-            build(1, n)
-            accs[0][...] += dot(grads[i], damp0[...])
-            build(0, jnp.minimum(n + 1, tiles * out_sub - 1))
-            accs[1][...] += dot(grads[i], damp1[...])
-            return carry
-
-        lax.fori_loop(0, out_sub, inner, 0)
-        x = acts[c // per, :, pl.ds(pl.multiple_of(lax.rem(c, per) * tile, tile), tile)].astype(F32)
-        for q in range(QUERIES):
-            product = accs[q][...] * x
-            total = product[:, 0:128]
-            for g in range(1, tile // 128):
-                total = total + product[:, g * 128 : (g + 1) * 128]
-            lanes[q] += total
+        build(1, c)
+        score(0, c)
+        build(0, jnp.minimum(c + 1, tiles - 1))
+        score(1, c)
         return carry
 
     build(0, 0)
@@ -263,8 +264,6 @@
             device_id=group_peer(k),
             device_id_type=MESH,
         ).wait_recv()
-    for copy in sends:
-        copy.wait_send()
     scores = jnp.sum(parts[...], axis=0)
     token_out[...] = scores
 
@@ -279,7 +278,6 @@
         found = jnp.where(lane == e, value, found)
         start = end
     sums[ex] = found
-    sends = []
     for k in range(1, exs):
         sends.append(
             pltpu.make_async_remote_copy(
@@ -302,9 +300,9 @@
             device_id={"ex": source},
             device_id_type=MESH,
         ).wait_recv()
-    for copy in sends:
+    example_out[...] = jnp.sum(sums[...], axis=0)[:, 0 : lengths.shape[0]]
+    for copy in firsts + forwards + sends:
         copy.wait_send()
-    example_out[...] = jnp.sum(sums[...], axis=0)[:, 0 : lengths.shape[0]]
 
 
 def solution(mesh):
@@ -329,9 +327,8 @@
         count = exs * held
         n_in, n_out = in_sub * width, out_sub * width
         levels = level_table.shape[0]
-        tile = width // 2
+        tile = width // 4
         group = rows * cols
-        ids = jnp.broadcast_to(query_ids[:, None], (held, 128))
         hbm = pl.BlockSpec(memory_space=pl.ANY)
         vmem = pl.BlockSpec(memory_space=pltpu.VMEM)
         smem = pl.BlockSpec(memory_space=pltpu.SMEM)
@@ -343,11 +340,11 @@
                 jax.ShapeDtypeStruct((QUERIES, tokens), F32),
                 jax.ShapeDtypeStruct((QUERIES, lengths.shape[0]), F32),
             ),
-            in_specs=[hbm] * 7 + [vmem] * 3 + [smem],
+            in_specs=[hbm] * 4 + [smem] + [hbm] * 2 + [vmem] * 3 + [smem],
             out_specs=(vmem, vmem),
             scratch_shapes=[
                 pltpu.VMEM((in_sub, tokens, width), BF16),
-                pltpu.VMEM((out_sub, tokens, width), BF16),
+                pltpu.VMEM((tokens, n_out), BF16),
                 pltpu.VMEM((in_sub, width, width), BF16),
                 pltpu.VMEM((out_sub, width, width), BF16),
                 pltpu.VMEM((count, n_in), BF16),
@@ -357,10 +354,8 @@
                 pltpu.VMEM((n_out, n_in), BF16),
                 pltpu.VMEM((n_out, count), BF16),
                 pltpu.VMEM((QUERIES, count, n_in), BF16),
-                pltpu.VMEM((width, tile), BF16),
-                pltpu.VMEM((width, tile), BF16),
-                pltpu.VMEM((tokens, tile), F32),
-                pltpu.VMEM((tokens, tile), F32),
+                pltpu.VMEM((n_out, tile), BF16),
+                pltpu.VMEM((n_out, tile), BF16),
                 pltpu.VMEM((QUERIES, tokens, 128), F32),
                 pltpu.VMEM((group, QUERIES, tokens), F32),
                 pltpu.VMEM((exs, QUERIES, 128), F32),
@@ -382,7 +377,7 @@
             train_out,
             query_in,
             query_out,
-            ids,
+            query_ids,
             in_basis,
             out_basis,
             level_table,

time: 73 us -> 66.9 us (0.916)
  Pallas kernels: 68.3 us -> 63.5 us
  local copies, waits for them, and re-layouts: 3.82 us -> 2.48 us
    pallas_call x1, Pallas kernels: 68.3 us -> 63.5 us  [body(): pl.pallas_call(functools.partial(kernel, (rows, cols, exs, tile)), out_sh...]
    broadcast_in_dim x1 -> x0, local copies, waits for them, and re-layouts: 1.33 us -> none  [body(): ids = jnp.broadcast_to(query_ids[:, None], (held, 128))]
where the time goes in v2:
time: 66.9 us; the launch traced here: 66.6 us
  Pallas kernels  63.5 us (95%)
  local copies, waits for them, and re-layouts  2.48 us (4%)
    pallas_call x1, Pallas kernels, body(): pl.pallas_call(functools.partial(kernel, (rows, cols, exs, tile)), out_sh...  63.5 us
    unnamed x2, local copies, waits for them, and re-layouts  2.48 us

profile of v2, /device:TPU:0, one launch (start us, length us, event | category | flops | bytes accessed | tf_op | source)
XLA Modules:
  0.0 66.6 jit_solution(17739000202187880258)
XLA Ops:
  0.6 63.5 %shard_map.122 = (f32[2,512]{1,0:T(2,128)}, f32[2,4]{1,0:T(2,128)}) custom-call(bf16[512,2048]{1,0:T(8,128)(2,1)} %train_in.1, bf16[512,4096]{1,0:T(8,128)(2,1)} %train_out.1, bf16[32,2048]{1,0:T(8,128)(2,1)} %query_in.1, bf16[32,4096]{1,0:T(8,128)(2,1)} %query_out.1, s32[32]{0:T(128)} %ids.1, bf16[2,1024,1024]{2,1,0:T(8,128)(2,1)} %in_basis.1, ...), custom_call_target="tpu_custom_call" | custom-call | tf_op jit(solution)/shard_map/pallas_call | solution.py:337
  64.1 1.3 %copy.15 = f32[2,512]{1,0:T(2,128)} copy(f32[2,512]{1,0:T(2,128)} %get-tuple-element.4) | data formatting | bytes 8192
  65.4 1.2 %copy.16 = f32[2,4]{1,0:T(2,128)} copy(f32[2,4]{1,0:T(2,128)} %get-tuple-element.5) | data formatting | bytes 64

commit v3 on v2

--- a/solution.py
+++ b/solution.py
@@ -327,7 +327,7 @@
         count = exs * held
         n_in, n_out = in_sub * width, out_sub * width
         levels = level_table.shape[0]
-        tile = width // 4
+        tile = width // 2 if 4 * count <= width else width // 4
         group = rows * cols
         hbm = pl.BlockSpec(memory_space=pl.ANY)
         vmem = pl.BlockSpec(memory_space=pltpu.VMEM)

time: 66.9 us -> 66.5 us (level)
  no operation moved by 1% of the time
where the time goes in v3:
time: 66.5 us; the launch traced here: 66.3 us
  Pallas kernels  63.2 us (95%)
  local copies, waits for them, and re-layouts  2.48 us (4%)
    pallas_call x1, Pallas kernels, body(): pl.pallas_call(functools.partial(kernel, (rows, cols, exs, tile)), out_sh...  63.2 us
    unnamed x2, local copies, waits for them, and re-layouts  2.48 us

profile of v3, /device:TPU:0, one launch (start us, length us, event | category | flops | bytes accessed | tf_op | source)
XLA Modules:
  0.0 66.3 jit_solution(1196352661043150652)
XLA Ops:
  0.6 63.2 %shard_map.122 = (f32[2,512]{1,0:T(2,128)}, f32[2,4]{1,0:T(2,128)}) custom-call(bf16[512,2048]{1,0:T(8,128)(2,1)} %train_in.1, bf16[512,4096]{1,0:T(8,128)(2,1)} %train_out.1, bf16[32,2048]{1,0:T(8,128)(2,1)} %query_in.1, bf16[32,4096]{1,0:T(8,128)(2,1)} %query_out.1, s32[32]{0:T(128)} %ids.1, bf16[2,1024,1024]{2,1,0:T(8,128)(2,1)} %in_basis.1, ...), custom_call_target="tpu_custom_call" | custom-call | tf_op jit(solution)/shard_map/pallas_call | solution.py:337
  63.8 1.3 %copy.15 = f32[2,512]{1,0:T(2,128)} copy(f32[2,512]{1,0:T(2,128)} %get-tuple-element.4) | data formatting | bytes 8192
  65.1 1.2 %copy.16 = f32[2,4]{1,0:T(2,128)} copy(f32[2,4]{1,0:T(2,128)} %get-tuple-element.5) | data formatting | bytes 64
